TPU v7x, 256 devices: a whole 4x4x8 slice. The times are simulated.
256 devices in a mesh: chan: 32 (over x_lo, z, core), stn: 8 (over x_hi, y).
Axes of the slice: x: 4 (x_hi: 2, x_lo: 2; x = x_hi * 2 + x_lo), y: 4, z: 8, core: 2. Of those that a mesh axis runs over, the one named last changes fastest.
Arguments:
- voltages: bfloat16 [32, 2, 1024, 512], P(None, None, ('stn', 'chan')), may hold values from -6 to 6
- phase_index: int32 [1024], P(('stn', 'chan')), may hold values from 0 to 1023
- int_lengths: int32 [4], replicated, may hold values from 1 to 192, 512 in all
- beam_weights: bfloat16 [2, 256, 1024], replicated, may hold values from -0.1875 to 0.1875
Outputs:
- visibilities: bfloat16 [8, 5, 4, 32, 2, 128, 128], P('stn', None, None, 'chan')
- beam_power: float32 [4, 32, 256], P(None, 'chan', 'stn')
Inputs may be any that keep to these rules, and one draw needn't show every extreme that they name: `int_lengths`: 4 integration lengths summing to 512; the longest is exactly 192.
All inputs are finite; a program needn't handle non-finite values.
Results may differ from a plain program's by a relative error of at most 0.0055.
Values may be sent and summed in bfloat16 or wider, within the bound.
A program may use at most 64 MiB of HBM per device.

v0:
```python
import math
import jax
import jax.numpy as jnp
from jax import lax
from jax.sharding import PartitionSpec as P

INTEG = 4
MOST = 192
BEAMS = 256
PHASES = 1024
full_turn = 2.0 * math.pi


def rotate(voltages, phase_index, channel):
    phase_turns = channel[:, None] * phase_index[None, :] % PHASES
    phase_angle = phase_turns.astype(jnp.float32) * (full_turn / PHASES)
    cosine = jnp.cos(phase_angle)[:, :, None]
    sine_part = jnp.sin(phase_angle)[:, :, None]
    real_in = voltages[:, 0].astype(jnp.float32)
    imag_in = voltages[:, 1].astype(jnp.float32)
    return jnp.stack(
        [real_in * cosine + imag_in * sine_part, imag_in * cosine - real_in * sine_part], axis=1
    ).astype(jnp.bfloat16)


def windows(block, starts, int_lengths):
    padded = jnp.pad(block, ((0, 0), (0, 0), (0, MOST)))
    in_range = jnp.arange(MOST, dtype=jnp.int32)
    result = []
    for period in range(INTEG):
        segment = lax.dynamic_slice_in_dim(padded, starts[period], MOST, 2)
        keep_mask = (in_range < int_lengths[period])[None, None, :]
        result.append(jnp.where(keep_mask, segment, jnp.zeros_like(segment)))
    return jnp.stack(result)


def correlate(own_parts, other, starts, int_lengths):
    padded = jnp.pad(other, ((0, 0), (0, 0), (0, MOST)))
    block_rows = own_parts.shape[2] // 2
    result = []
    for period in range(INTEG):
        segment = lax.dynamic_slice_in_dim(padded, starts[period], MOST, 2)
        products = jnp.einsum(
            "cal,cbl->cab", own_parts[period], segment, preferred_element_type=jnp.float32
        )
        real_part = products[:, :block_rows, :block_rows] + products[:, block_rows:, block_rows:]
        imag_part = products[:, block_rows:, :block_rows] - products[:, :block_rows, block_rows:]
        inverse = 1.0 / int_lengths[period].astype(jnp.float32)
        result.append((jnp.stack([real_part, imag_part], axis=1) * inverse).astype(jnp.bfloat16))
    return jnp.stack(result)


def stack_weights(beam_weights, beam_first, beam_count, column_first, column_count):
    weight_real = lax.dynamic_slice(
        beam_weights[0], (beam_first, column_first), (beam_count, column_count)
    )
    weight_imag = lax.dynamic_slice(
        beam_weights[1], (beam_first, column_first), (beam_count, column_count)
    )
    upper = jnp.concatenate([weight_real, -weight_imag], axis=1)
    lower = jnp.concatenate([weight_imag, weight_real], axis=1)
    return jnp.concatenate([upper, lower], axis=0)


def integrate(power, starts, int_lengths, form):
    samples = power.shape[-1]
    sample_index = jnp.arange(samples, dtype=jnp.int32)[None, :]
    in_window = (
        (sample_index >= starts[:, None]) & (sample_index < (starts + int_lengths)[:, None])
    ).astype(jnp.float32)
    summed = jnp.einsum(form, power, in_window, precision=lax.Precision.HIGHEST)
    return summed / int_lengths.astype(jnp.float32)[:, None, None]


def local(voltages, phase_index, int_lengths, beam_weights):
    channel = jnp.arange(voltages.shape[0], dtype=jnp.int32)
    rotated = rotate(voltages, phase_index, channel)
    turned = lax.all_to_all(rotated, "chan", split_axis=0, concat_axis=2, tiled=True)
    station = lax.axis_index("stn")
    stations = lax.axis_size("stn")
    halfway = stations // 2
    share = BEAMS // stations
    ch_local, _, block_rows, samples = turned.shape
    own = turned.reshape(ch_local, 2 * block_rows, samples)
    starts = jnp.cumsum(int_lengths) - int_lengths
    own_parts = windows(own, starts, int_lengths)

    def place(vis_total, other, offset):
        fresh = correlate(own_parts, other, starts, int_lengths)
        return lax.dynamic_update_slice(vis_total, fresh[None], (offset, 0, 0, 0, 0, 0))

    def leave(vis_total, other, offset):
        return vis_total

    vis_start = jnp.zeros((halfway + 1, INTEG, ch_local, 2, block_rows, block_rows), jnp.bfloat16)
    beam_start = jnp.zeros((ch_local, 2 * share, samples), jnp.float32)
    portion = lax.all_gather(turned, "stn", axis=2, tiled=True)
    first_row = jnp.int32(0)
    vis_total = vis_start
    beam_total = beam_start
    for member in range(portion.shape[2] // block_rows):
        other = portion[:, :, member * block_rows : (member + 1) * block_rows, :].reshape(
            ch_local, 2 * block_rows, samples
        )
        other_index = first_row // block_rows + member
        offset = (other_index - station) % stations
        vis_total = lax.cond(offset <= halfway, place, leave, vis_total, other, offset)
        stacked = stack_weights(
            beam_weights, station * share, share, other_index * block_rows, block_rows
        )
        partial_beam = jnp.einsum("rk,ckt->crt", stacked, other, preferred_element_type=jnp.float32)
        beam_total = beam_total + lax.optimization_barrier(
            partial_beam.astype(jnp.bfloat16)
        ).astype(jnp.float32)
    vis_total, beam_total = (vis_total, beam_total)
    beam_total = beam_total.reshape(ch_local, 2, share, samples)
    power = beam_total[:, 0] ** 2 + beam_total[:, 1] ** 2
    beam_power = integrate(power, starts, int_lengths, "cbt,jt->jcb")
    return (vis_total[None], beam_power)


def solution(mesh):
    return jax.shard_map(
        local,
        mesh=mesh,
        in_specs=(P(None, None, ("stn", "chan"), None), P(("stn", "chan")), P(), P()),
        out_specs=(P("stn", None, None, "chan", None, None, None), P(None, "chan", "stn")),
        check_vma=False,
    )
```

profile of v0, /device:TPU:1, one launch (start us, length us, event | category | flops | bytes accessed | tf_op | source)
XLA Modules:
  0.0 167.8 jit_solution(5252909715909642435)
XLA Ops:
  7.2 0.8 fusion.347
  8.2 1.2 fusion.273
  9.6 22.5 %all_to_all.18 = bf16[32,2,4,512]{3,2,1,0:T(4,128)(2,1)S(1)} all-to-all(bf16[32,2,4,512]{3,2,1,0:T(4,128)(2,1)S(1)} %pad_maximum_fusion), channel_id=1, replica_groups=mesh['chan'=32,'stn'=8] {'chan'}, dimensions={0} | all-to-all | bytes 524288 | tf_op jit(solution)/shard_map/all_to_all | solution.py:78
  32.2 0.8 all_to_all.16
  33.2 0.6 fusion.384
  40.9 0.6 fusion.383
  41.5 1.2 iota_compare_fusion.3
  42.7 1.1 iota_compare_fusion.5
  44.0 0.3 fusion.279
  44.3 44.1 %all-gather.2.cloned.1.call-done = bf16[1,2,1024,512]{3,2,1,0:T(8,128)(2,1)} async-done(((bf16[1,2,128,512]{3,2,1,0:T(8,128)(2,1)}), bf16[1,2,1024,512]{3,2,1,0:T(8,128)(2,1)}) %all-gather.2.cloned.1.call-update) | async-done | bytes 2097168 | tf_op jit(solution)/shard_map/all_gather | solution.py:97
  88.4 1.7 %fusion.380 = (bf16[1,2,128,512]{3,2,1,0:T(8,128)(2,1)S(1)}, bf16[1,2,128,512]{3,2,1,0:T(8,128)(2,1)S(1)}, bf16[1,2,128,512]{3,2,1,0:T(8,128)(2,1)S(1)}, bf16[1,...) fusion(bf16[1,2,1024,512]{3,2,1,0:T(8,128)(2,1)} %all-gather.2., ...), kind=kLoop, calls=%fused_computation.561 | loop fusion | bytes 4194304 | tf_op jit(solution)/shard_map/slice | solution.py:102
  91.4 13.8 %conditional.8 = (bf16[5,4,1,2,128,128]{4,5,3,1,2,0:T(8,128)(2,1)}) conditional(s32[]{:T(128)} %convert_element_type.674, () %tuple.58, (bf16[1,2,128,512]{3,2,1,0:T(8,128)(2,1)S(1)}, s32[4]{0:T(128)S(1)}, bf16[1,256,192]{2,1,0:T(8,128)(2,1)S(1)}, s32[4]{0:T(128)S(1)}, bf16[1,256,192]{2,1,0:T(8,128)(2,1)S(1)}, ...), branch_computations={%region_1.2_spmd, %region_2.3_spmd} | conditional | flops 102236168 | bytes 6685032 | solution.py:107
  91.5 0.7 fusion.364
  93.8 0.2 convolution_bitcast_fusion.2
  103.1 1.4 broadcast_in_dim.57
  104.5 0.7 fusion
  105.2 13.0 %conditional.9 = (bf16[5,4,1,2,128,128]{4,5,3,1,2,0:T(8,128)(2,1)}) conditional(s32[]{:T(128)} %convert_element_type.673, bf16[5,4,1,2,128,128]{4,5,3,1,2,0:T(8,128)(2,1)} %get-tuple-element.511, (bf16[1,2,128,512]{3,2,1,0:T(8,128)(2,1)S(1)}, s32[4]{0:T(128)S(1)}, bf16[1,256,192]{2,1,0:T(8,128)(2,1)S(1)}, s32[4]{0:T(128)S(1)}, ...), branch_computations={%region_3.4_spmd, %region_4.5_spmd} | conditional | flops 102236168 | bytes 5374310 | solution.py:107
  105.2 0.7 fusion.366
  117.5 0.7 fusion.33
  118.2 13.0 %conditional.10 = (bf16[5,4,1,2,128,128]{4,5,3,1,2,0:T(8,128)(2,1)}) conditional(s32[]{:T(128)} %convert_element_type.672, bf16[5,4,1,2,128,128]{4,5,3,1,2,0:T(8,128)(2,1)} %get-tuple-element.512, (bf16[1,2,128,512]{3,2,1,0:T(8,128)(2,1)S(1)}, s32[4]{0:T(128)S(1)}, bf16[1,256,192]{2,1,0:T(8,128)(2,1)S(1)}, s32[4]{0:T(128)S(1)}, ...), branch_computations={%region_5.6_spmd, %region_6.7_spmd} | conditional | flops 102236168 | bytes 5374310 | solution.py:107
  118.2 0.7 fusion.368
  130.5 0.7 fusion.66
  131.2 13.0 %conditional.11 = (bf16[5,4,1,2,128,128]{4,5,3,1,2,0:T(8,128)(2,1)}) conditional(s32[]{:T(128)} %convert_element_type.671, bf16[5,4,1,2,128,128]{4,5,3,1,2,0:T(8,128)(2,1)} %get-tuple-element.513, (bf16[1,2,128,512]{3,2,1,0:T(8,128)(2,1)S(1)}, s32[4]{0:T(128)S(1)}, bf16[1,256,192]{2,1,0:T(8,128)(2,1)S(1)}, s32[4]{0:T(128)S(1)}, ...), branch_computations={%region_7.8_spmd, %region_8.9_spmd} | conditional | flops 102236168 | bytes 5374310 | solution.py:107
  131.2 0.7 fusion.370
  143.5 0.7 fusion.99
  144.2 13.0 %conditional.12 = (bf16[5,4,1,2,128,128]{4,5,3,1,2,0:T(8,128)(2,1)}) conditional(s32[]{:T(128)} %convert_element_type.670, bf16[5,4,1,2,128,128]{4,5,3,1,2,0:T(8,128)(2,1)} %get-tuple-element.514, (bf16[1,2,128,512]{3,2,1,0:T(8,128)(2,1)S(1)}, s32[4]{0:T(128)S(1)}, bf16[1,256,192]{2,1,0:T(8,128)(2,1)S(1)}, s32[4]{0:T(128)S(1)}, ...), branch_computations={%region_9.10_spmd, %region_10.11_spmd} | conditional | flops 102236168 | bytes 5374310 | solution.py:107
  144.2 0.7 fusion.372
  156.5 0.7 fusion.132
  157.3 0.8 convolution_divide_fusion
  158.1 1.8 %conditional.15 = (bf16[1,5,4,1,2,128,128]{6,5,4,3,2,1,0:T(8,128)(2,1)S(1)}) conditional(s32[]{:T(128)} %convert_element_type.667, bf16[5,4,1,2,128,128]{4,5,3,1,0,2:T(8,128)(2,1)} %bitcast.320, (bf16[5,4,1,2,128,128]{4,5,3,1,2,0:T(8,128)(2,1)}, bf16[1,2,128,512]{3,2,1,0:T(8,128)(2,1)S(1)}, s32[4]{0:T(128)S(1)}, ...), branch_computations={%region_15.16_spmd, %region_16.17_spmd} | conditional | flops 102236168 | bytes 7995750 | solution.py:107
  158.1 1.8 %copy.20 = bf16[1,5,4,1,2,128,128]{6,5,4,3,2,1,0:T(8,128)(2,1)S(1)} copy(bf16[1,5,4,1,2,128,128]{5,6,4,2,3,1,0:T(8,128)(2,1)} %bitcast.266) | data formatting | bytes 2621440 | tf_op jit(solution)/shard_map/cond
  159.9 1.0 copy-done
  (87 shorter events, 7.5 us)
Async XLA Ops:
  7.2 81.2 %all-gather.2.cloned.1.call-start = ((), (), s32[]{:S(2)}) async-start(), calls=%async_computation.1 | async-start | bytes 2359296 | tf_op jit(solution)/shard_map/all_gather | solution.py:97
  9.4 23.6 %copy-start.2 = (s32[4]{0:T(128)S(1)}, s32[4]{0:T(128)}, u32[]{:S(2)}) copy-start(s32[4]{0:T(128)} %param.22) | copy-start | bytes 52
  9.4 34.4 %copy-start.1 = (bf16[2,256,1024]{2,1,0:T(8,128)(2,1)S(1)}, bf16[2,256,1024]{2,1,0:T(8,128)(2,1)}, u32[]{:S(2)}) copy-start(bf16[2,256,1024]{2,1,0:T(8,128)(2,1)} %param.23) | copy-start | bytes 3145732
  159.9 1.1 copy-start
Sparse Core Ops, SparseCore 0:
  33.1 55.2 all-gather.1
where the time goes:
time: 169 us; the launch traced here: 168 us
  loops' own time  52 us (31%)
  waiting for transfers between devices  44.1 us (26%)
  blocking collectives  22.5 us (13%)
  between operations  21.3 us (13%)
  local copies, waits for them, and re-layouts  11.7 us (7%)
  other arithmetic  9.31 us (6%)
  matrix products  6.89 us (4%)
    another operation x8, loops' own time, local(): lax.cond(offset <= halfway, place, leave, vis_total, other, offset)  52 us
    all_gather x1, waiting for transfers between devices, local(): portion = lax.all_gather(turned, 'stn', axis=2, tiled=True)  44.1 us
    all_to_all x1, blocking collectives, local(): lax.all_to_all(rotated, 'chan', split_axis=0, concat_axis=2, tiled=True)  22.5 us
    dot_general x20, matrix products, correlate(): jnp.einsum('cal,cbl->cab', own_parts[period], segment, preferred_element_...  4.83 us
    dynamic_update_slice x5, other arithmetic, place(): lax.dynamic_update_slice(vis_total, fresh[None], (offset, 0, 0, 0, 0, 0))  3.64 us
    slice x5, local copies, waits for them, and re-layouts, correlate(): inverse = 1.0 / int_lengths[period].astype(jnp.float32)  3.38 us
  transfers between devices with their start and end apart: 1, of which 1 were waited for; matrix products, arithmetic and copies ran while one was open for 3% of the time, Pallas kernels for 0%

commit v1 on v0

--- a/solution.py
+++ b/solution.py
@@ -94,7 +94,9 @@
 
     vis_start = jnp.zeros((halfway + 1, INTEG, ch_local, 2, block_rows, block_rows), jnp.bfloat16)
     beam_start = jnp.zeros((ch_local, 2 * share, samples), jnp.float32)
-    portion = lax.all_gather(turned, "stn", axis=2, tiled=True)
+    portion = jnp.concatenate(
+        lax.all_to_all(jnp.stack([turned] * lax.axis_size("stn")), "stn", 0, 0), axis=2
+    )
     first_row = jnp.int32(0)
     vis_total = vis_start
     beam_total = beam_start

time: 169 us -> 132 us (0.78)
  waiting for transfers between devices: 44.1 us -> 11.2 us
  between operations: 21.3 us -> 8.9 us
  starting transfers between devices: 0.04 us -> 6.49 us
  other arithmetic: 9.31 us -> 11.9 us
    all_gather x1 -> x0, waiting for transfers between devices: 44.1 us -> none  [local(): portion = lax.all_gather(turned, 'stn', axis=2, tiled=True)]
    all_to_all x0 -> x1, waiting for transfers between devices: none -> 11.2 us  [local(): lax.all_to_all(jnp.stack([turned] * lax.axis_size('stn')), 'stn', 0, 0)]
    all_to_all x0 -> x1, starting transfers between devices: none -> 6.49 us  [local(): lax.all_to_all(jnp.stack([turned] * lax.axis_size('stn')), 'stn', 0, 0)]
  transfers between devices with their start and end apart: 1 -> 1, of which waited for: 1 -> 1; matrix products, arithmetic and copies ran while one was open for 3% -> 5% of each run, Pallas kernels for 0% -> 0%
where the time goes in v1:
time: 132 us; the launch traced here: 131 us
  loops' own time  50.7 us (38%)
  blocking collectives  22.4 us (17%)
  local copies, waits for them, and re-layouts  12.5 us (9%)
  other arithmetic  11.9 us (9%)
  waiting for transfers between devices  11.2 us (8%)
  between operations  8.9 us (7%)
  matrix products  6.88 us (5%)
  starting transfers between devices  6.49 us (5%)
    another operation x8, loops' own time, local(): lax.cond(offset <= halfway, place, leave, vis_total, other, offset)  50.7 us
    all_to_all x1, blocking collectives, local(): lax.all_to_all(rotated, 'chan', split_axis=0, concat_axis=2, tiled=True)  22.4 us
    all_to_all x1, waiting for transfers between devices, local(): lax.all_to_all(jnp.stack([turned] * lax.axis_size('stn')), 'stn', 0, 0)  11.2 us
    all_to_all x1, starting transfers between devices, local(): lax.all_to_all(jnp.stack([turned] * lax.axis_size('stn')), 'stn', 0, 0)  6.49 us
    dot_general x20, matrix products, correlate(): jnp.einsum('cal,cbl->cab', own_parts[period], segment, preferred_element_...  4.83 us
    lt x2, other arithmetic, windows(): keep_mask = (in_range < int_lengths[period])[None, None, :]  3.72 us
    dynamic_update_slice x5, other arithmetic, place(): lax.dynamic_update_slice(vis_total, fresh[None], (offset, 0, 0, 0, 0, 0))  3.64 us
    slice x5, local copies, waits for them, and re-layouts, correlate(): inverse = 1.0 / int_lengths[period].astype(jnp.float32)  3.32 us
  transfers between devices with their start and end apart: 1, of which 1 were waited for; matrix products, arithmetic and copies ran while one was open for 5% of the time, Pallas kernels for 0%

profile of v1, /device:TPU:1, one launch (start us, length us, event | category | flops | bytes accessed | tf_op | source)
XLA Modules:
  0.0 130.9 jit_solution(6628900193765690310)
XLA Ops:
  0.6 0.8 fusion.347
  1.6 1.2 fusion.273
  3.0 22.4 %all_to_all.20 = bf16[32,2,4,512]{3,2,1,0:T(4,128)(2,1)S(1)} all-to-all(bf16[32,2,4,512]{3,2,1,0:T(4,128)(2,1)S(1)} %pad_maximum_fusion), channel_id=1, replica_groups=mesh['chan'=32,'stn'=8] {'chan'}, dimensions={0} | all-to-all | bytes 524288 | tf_op jit(solution)/shard_map/all_to_all | solution.py:78
  25.6 1.5 %stack.365 = bf16[8,1,2,128,512]{4,3,2,1,0:T(8,128)(2,1)} broadcast(bf16[2,128,512]{2,1,0:T(8,128)(2,1)S(1)} %copy.36), dimensions={2,3,4} | broadcast | bytes 2359296 | tf_op jit(solution)/shard_map/stack | solution.py:98
  27.1 6.5 %all-to-all-start.1 = ((bf16[8,1,2,128,512]{4,3,2,1,0:T(8,128)(2,1)}), bf16[8,1,2,128,512]{4,3,2,1,0:T(8,128)(2,1)S(1)}, u32[]{:S(2)}, u32[]{:S(2)}) async-start(bf16[8,1,2,128,512]{4,3,2,1,0:T(8,128)(2,1)} %stack.365), calls=%async_computation.1 | async-start | bytes 4194304 | tf_op jit(solution)/shard_map/all_to_all | solution.py:98
  33.8 0.6 fusion.382
  34.4 0.7 fusion.384
  43.0 0.7 fusion.383
  43.7 1.8 %iota_compare_fusion.3 = (pred[192]{0:T(512)(128)(4,1)}, pred[192]{0:T(512)(128)(4,1)}) fusion(s32[]{:T(128)} %bitcast.321, s32[]{:T(128)} %bitcast.319), kind=kLoop, calls=%fused_computation.522 | loop fusion | flops 384 | bytes 392 | tf_op jit(solution)/shard_map/lt | solution.py:32
  45.5 1.9 %iota_compare_fusion.5 = (pred[192]{0:T(512)(128)(4,1)}, pred[192]{0:T(512)(128)(4,1)}) fusion(s32[]{:T(128)} %bitcast.317, s32[]{:T(128)} %bitcast.314), kind=kLoop, calls=%fused_computation.524 | loop fusion | flops 384 | bytes 392 | tf_op jit(solution)/shard_map/lt | solution.py:32
  47.5 0.6 fusion.356
  48.7 11.2 %all-to-all-done.1 = bf16[8,1,2,128,512]{4,3,2,1,0:T(8,128)(2,1)S(1)} async-done(((bf16[8,1,2,128,512]{4,3,2,1,0:T(8,128)(2,1)}), bf16[8,1,2,128,512]{4,3,2,1,0:T(8,128)(2,1)S(1)}, u32[]{:S(2)}, u32[]{:S(2)}) %all-to-all-start.1) | async-done | bytes 2097184 | tf_op jit(solution)/shard_map/all_to_all | solution.py:98
  62.1 14.3 %conditional.8 = (bf16[5,4,1,2,128,128]{4,5,3,1,2,0:T(8,128)(2,1)}) conditional(s32[]{:T(128)} %convert_element_type.674, () %tuple.58, (bf16[1,2,128,512]{3,2,1,0:T(8,128)(2,1)S(1)}, s32[4]{0:T(128)S(1)}, bf16[1,256,192]{2,1,0:T(8,128)(2,1)S(1)}, s32[4]{0:T(128)S(1)}, bf16[1,256,192]{2,1,0:T(8,128)(2,1)S(1)}, ...), branch_computations={%region_1.2_spmd, %region_2.3_spmd} | conditional | flops 102236168 | bytes 6685032 | solution.py:109
  62.2 0.7 fusion.364
  74.3 1.4 %broadcast_in_dim.57 = bf16[5,4,1,2,128,128]{4,5,3,1,2,0:T(8,128)(2,1)} broadcast(bf16[]{:T(256)} %constant.228.clone), dimensions={} | broadcast | bytes 1310722 | tf_op jit(solution)/shard_map/broadcast_in_dim | solution.py:95
  75.7 0.7 fusion
  76.4 12.6 %conditional.9 = (bf16[5,4,1,2,128,128]{4,5,3,1,2,0:T(8,128)(2,1)}) conditional(s32[]{:T(128)} %convert_element_type.673, bf16[5,4,1,2,128,128]{4,5,3,1,2,0:T(8,128)(2,1)} %get-tuple-element.544, (bf16[1,2,128,512]{3,2,1,0:T(8,128)(2,1)S(1)}, s32[4]{0:T(128)S(1)}, bf16[1,256,192]{2,1,0:T(8,128)(2,1)S(1)}, s32[4]{0:T(128)S(1)}, ...), branch_computations={%region_3.4_spmd, %region_4.5_spmd} | conditional | flops 102236168 | bytes 5374310 | solution.py:109
  76.4 0.7 fusion.366
  88.2 0.7 fusion.33
  89.0 12.6 %conditional.10 = (bf16[5,4,1,2,128,128]{4,5,3,1,2,0:T(8,128)(2,1)}) conditional(s32[]{:T(128)} %convert_element_type.672, bf16[5,4,1,2,128,128]{4,5,3,1,2,0:T(8,128)(2,1)} %get-tuple-element.545, (bf16[1,2,128,512]{3,2,1,0:T(8,128)(2,1)S(1)}, s32[4]{0:T(128)S(1)}, bf16[1,256,192]{2,1,0:T(8,128)(2,1)S(1)}, s32[4]{0:T(128)S(1)}, ...), branch_computations={%region_5.6_spmd, %region_6.7_spmd} | conditional | flops 102236168 | bytes 5374310 | solution.py:109
  89.0 0.7 fusion.368
  100.8 0.7 fusion.66
  101.5 12.6 %conditional.11 = (bf16[5,4,1,2,128,128]{4,5,3,1,2,0:T(8,128)(2,1)}) conditional(s32[]{:T(128)} %convert_element_type.671, bf16[5,4,1,2,128,128]{4,5,3,1,2,0:T(8,128)(2,1)} %get-tuple-element.546, (bf16[1,2,128,512]{3,2,1,0:T(8,128)(2,1)S(1)}, s32[4]{0:T(128)S(1)}, bf16[1,256,192]{2,1,0:T(8,128)(2,1)S(1)}, s32[4]{0:T(128)S(1)}, ...), branch_computations={%region_7.8_spmd, %region_8.9_spmd} | conditional | flops 102236168 | bytes 5374310 | solution.py:109
  101.5 0.7 fusion.370
  113.3 0.7 fusion.99
  114.1 12.6 %conditional.12 = (bf16[5,4,1,2,128,128]{4,5,3,1,2,0:T(8,128)(2,1)}) conditional(s32[]{:T(128)} %convert_element_type.670, bf16[5,4,1,2,128,128]{4,5,3,1,2,0:T(8,128)(2,1)} %get-tuple-element.547, (bf16[1,2,128,512]{3,2,1,0:T(8,128)(2,1)S(1)}, s32[4]{0:T(128)S(1)}, bf16[1,256,192]{2,1,0:T(8,128)(2,1)S(1)}, s32[4]{0:T(128)S(1)}, ...), branch_computations={%region_9.10_spmd, %region_10.11_spmd} | conditional | flops 102236168 | bytes 5374310 | solution.py:109
  114.1 0.7 fusion.372
  125.9 0.7 fusion.132
  127.3 0.8 convolution_divide_fusion
  128.1 1.8 %conditional.15 = (bf16[1,5,4,1,2,128,128]{6,5,4,3,2,1,0:T(8,128)(2,1)S(1)}) conditional(s32[]{:T(128)} %convert_element_type.667, bf16[5,4,1,2,128,128]{4,5,3,1,0,2:T(8,128)(2,1)} %bitcast.324, (bf16[5,4,1,2,128,128]{4,5,3,1,2,0:T(8,128)(2,1)}, bf16[1,2,128,512]{3,2,1,0:T(8,128)(2,1)S(1)}, s32[4]{0:T(128)S(1)}, ...), branch_computations={%region_15.16_spmd, %region_16.17_spmd} | conditional | flops 102236168 | bytes 7995750 | solution.py:109
  128.1 1.8 %copy.43 = bf16[1,5,4,1,2,128,128]{6,5,4,3,2,1,0:T(8,128)(2,1)S(1)} copy(bf16[1,5,4,1,2,128,128]{5,6,4,2,3,1,0:T(8,128)(2,1)} %bitcast.266) | data formatting | bytes 2621440 | tf_op jit(solution)/shard_map/cond
  129.9 1.0 copy-done
  (117 shorter events, 9.6 us)
Async XLA Ops:
  27.1 6.5 %copy-start.2 = (s32[4]{0:T(128)S(1)}, s32[4]{0:T(128)}, u32[]{:S(2)}) copy-start(s32[4]{0:T(128)} %param.22) | copy-start | bytes 52
  27.1 20.2 %copy-start.1 = (bf16[2,256,1024]{2,1,0:T(8,128)(2,1)S(1)}, bf16[2,256,1024]{2,1,0:T(8,128)(2,1)}, u32[]{:S(2)}) copy-start(bf16[2,256,1024]{2,1,0:T(8,128)(2,1)} %param.23) | copy-start | bytes 3145732
  27.1 32.7 %all-to-all-start.1 = ((bf16[8,1,2,128,512]{4,3,2,1,0:T(8,128)(2,1)}), bf16[8,1,2,128,512]{4,3,2,1,0:T(8,128)(2,1)S(1)}, u32[]{:S(2)}, u32[]{:S(2)}) async-start(bf16[8,1,2,128,512]{4,3,2,1,0:T(8,128)(2,1)} %stack.365), calls=%async_computation.1 | async-start | bytes 4194304 | tf_op jit(solution)/shard_map/all_to_all | solution.py:98
  33.8 13.6 %copy-start.14 = (s32[4,1]{0,1:T(1,128)}, s32[4,1]{0,1:T(1,128)S(1)}, u32[]{:S(2)}) copy-start(s32[4,1]{0,1:T(1,128)S(1)} %reduce-window.8) | copy-start | bytes 52
  47.5 0.9 copy-start.10
  47.5 0.9 copy-start.11
  47.5 0.9 copy-start.12
  47.5 0.9 copy-start.13
  60.0 0.7 copy-start.8
  60.1 0.7 copy-start.9
  60.1 0.9 copy-start.6
  60.1 0.9 copy-start.7
  60.1 1.0 copy-start.4
  60.1 1.0 copy-start.5
  60.1 1.2 copy-start.3
  126.6 0.6 copy-start.15
  126.6 0.7 copy-start.16
  129.9 1.1 copy-start
